TPU v7x, 32 devices: a whole 2x2x4 slice. The times are simulated.
32 devices in a mesh: ex: 4 (over z), ctx: 8 (over y, x, core).
Axes of the slice: x: 2, y: 2, z: 4, core: 2. Of those that a mesh axis runs over, the one named last changes fastest.
Arguments:
- stream: bfloat16 [4, 256, 8192], P('ex', None, 'ctx'), may hold values from -6 to 6
- cotangent: bfloat16 [4, 256, 8192], P('ex', None, 'ctx'), may hold values from -6 to 6
- base_ids: int32 [4, 8192], P('ex', 'ctx'), may hold values from 0 to 4
- clip_bound: int32 [4], P('ex'), may hold values from 1 to 4
- w_value: bfloat16 [256, 256], replicated, may hold values from -2 to 2
- w_gate: bfloat16 [256, 256], replicated, may hold values from -0.375 to 0.375
- filter_taps: float32 [256, 8192], P('ctx', 'ex'), may hold values from -0.0625 to 0.0625
- filter_bias: float32 [256], P('ctx'), may hold values from 0.1 to 1.9
Outputs:
- input_grad: bfloat16 [4, 256, 8192], P('ex', None, 'ctx')
- filter_grad: float32 [256, 8192], P('ctx', 'ex')
All inputs are finite; a program needn't handle non-finite values.
Results may differ from a plain program's by a relative error of at most 0.015.
Values may be sent and summed in bfloat16 or wider, within the bound.
A program may use at most 128 MiB of HBM per device.

v0:
```python
import functools
import math

import jax
import jax.numpy as jnp
import numpy as np
from jax import lax
from jax.experimental import pallas as pl
from jax.experimental.pallas import tpu as pltpu
from jax.sharding import PartitionSpec as P

LANES = 128
UNKNOWN = 4
EPS = 1e-06
F32 = jnp.float32
BF16 = jnp.bfloat16
MESH = pl.DeviceIdType.MESH


def tables(rows):
    whole = 2 * rows * LANES
    ka = np.arange(rows) + 0.5
    a = np.arange(rows)
    r = np.arange(LANES)
    outer = 2 * math.pi * ka[:, None] * a[None, :] / (2 * rows)
    inner = 2 * math.pi * (r[:, None] * r[None, :] % LANES) / LANES
    twist = 2 * math.pi * ka[:, None] * r[None, :] / whole
    cos, sin = np.cos(inner), np.sin(inner)
    first = np.concatenate([np.cos(outer), -np.sin(outer)], 0)
    last = np.concatenate([np.cos(outer).T, -np.sin(outer).T], 1)
    second = np.block([[cos, -sin], [sin, cos]])
    third = np.block([[cos, sin], [-sin, cos]])
    twist = np.stack([np.cos(twist), np.sin(twist)])
    return (
        jnp.asarray(first, BF16),
        jnp.asarray(second, BF16),
        jnp.asarray(third, BF16),
        jnp.asarray(last, BF16),
        jnp.asarray(twist, F32),
    )


def dot(x, y):
    return jnp.dot(x, y, preferred_element_type=F32)


def stack_rows(blocks):
    if blocks[0].shape[0] % 16 == 0:
        return jnp.concatenate(blocks, 0)
    return jnp.concatenate([b.astype(F32) for b in blocks], 0).astype(BF16)


def kernel(
    n_ctx, n_ex, halves, group,
    stream, cotangent, ids, bound, w_value, w_gate, taps, bias,
    first, second, third, last, twist,
    input_grad, filter_grad,
    in_send, in_recv, out_send, out_recv, tap_send, tap_recv, grad_send, grad_recv,
    sq_send, sq_recv, fac_send, fac_recv,
    val_wide, sig_wide, fil_wide, conv_wide, back_wide, tapg_wide,
    in_ss, in_rs, out_ss, out_rs, tap_ss, tap_rs, grad_ss, grad_rs,
    sq_ss, sq_rs, fac_ss, fac_rs,
):
    ex = lax.axis_index("ex")
    ctx = lax.axis_index("ctx")
    ctx_peers = [lax.rem(ctx + i, n_ctx) for i in range(1, n_ctx)]
    ex_peers = [lax.rem(ex + i, n_ex) for i in range(1, n_ex)]
    depth = stream.shape[1]
    tokens = stream.shape[2]
    chans = taps.shape[0]
    part = chans // halves
    tiles = tokens // LANES
    rows = n_ctx * tiles
    lag_tiles = rows // n_ex

    def to_ctx(src, dst, ss, rs, peer):
        return pltpu.make_async_remote_copy(
            src_ref=src, dst_ref=dst, send_sem=ss, recv_sem=rs,
            device_id=(ex, peer), device_id_type=MESH,
        )

    def to_ex(src, dst, ss, rs, peer):
        return pltpu.make_async_remote_copy(
            src_ref=src, dst_ref=dst, send_sem=ss, recv_sem=rs,
            device_id=(peer, ctx), device_id_type=MESH,
        )

    barrier = pltpu.get_barrier_semaphore()
    for peer in ctx_peers:
        pl.semaphore_signal(barrier, inc=1, device_id=(ex, peer), device_id_type=MESH)
    for peer in ex_peers:
        pl.semaphore_signal(barrier, inc=1, device_id=(peer, ctx), device_id_type=MESH)

    tap_send[...] = taps[...].astype(BF16)
    keep = ids[...] != UNKNOWN

    width = min(256, tokens)
    tok = stream[0]
    for lo in range(0, tokens, width):
        cols = slice(lo, lo + width)
        value = dot(w_value[...], tok[:, cols])
        gate = dot(w_gate[...], tok[:, cols]).astype(BF16).astype(F32)
        cot = jnp.where(keep[:, cols], cotangent[0, :, cols].astype(F32), 0.0)
        signal = gate * cot
        for d in range(n_ctx):
            for h in range(halves):
                at = d * chans + h * part
                in_send[h, d, 0, :, cols] = value[at:at + part].astype(BF16)
                in_send[h, d, 1, :, cols] = signal[at:at + part].astype(BF16)

    pl.semaphore_wait(barrier, n_ctx - 1 + n_ex - 1)
    for peer in ex_peers:
        to_ex(tap_send, tap_recv.at[ex], tap_ss.at[peer], tap_rs.at[ex], peer).start()
    for h in range(halves):
        for peer in ctx_peers:
            to_ctx(
                in_send.at[h, peer], in_recv.at[h, ctx],
                in_ss.at[h, peer], in_rs.at[h, ctx], peer,
            ).start()
    tap_recv[ex] = tap_send[...]
    for h in range(halves):
        in_recv[h, ctx] = in_send[h, ctx]
    for peer in ex_peers:
        to_ex(tap_send, tap_recv.at[peer], tap_ss.at[peer], tap_rs.at[peer], peer).wait_recv()

    g_first, g_second, g_third, g_last = first[...], second[...], third[...], last[...]
    scale = 1.0 / (rows * LANES)
    square = jnp.zeros((8, LANES), F32)

    for h in range(halves):
        chan_lo = h * part
        for e in range(n_ex):
            for j in range(lag_tiles):
                at = (e * lag_tiles + j) * part
                fil_wide[at:at + part, :] = tap_recv[
                    e, chan_lo:chan_lo + part, j * LANES:(j + 1) * LANES
                ].astype(F32)
        for peer in ctx_peers:
            to_ctx(
                in_send.at[h, peer], in_recv.at[h, peer],
                in_ss.at[h, peer], in_rs.at[h, peer], peer,
            ).wait_recv()
        for d in range(n_ctx):
            for j in range(tiles):
                at = (d * tiles + j) * part
                cols = slice(j * LANES, (j + 1) * LANES)
                val_wide[at:at + part, :] = in_recv[h, d, 0, :, cols].astype(F32)
                sig_wide[at:at + part, :] = in_recv[h, d, 1, :, cols].astype(F32)

        def some_channels(step, carry):
            base = step * group
            pick = lambda c: pl.ds(base + c, rows, stride=part)
            flat = []
            for c in range(group):
                for ref in (fil_wide, val_wide, sig_wide):
                    flat.append(ref[pick(c), :].astype(BF16))
            mid = dot(g_first, jnp.concatenate(flat, 1))
            t_cos, t_sin = twist[0], twist[1]
            blocks = []
            for m in range(3 * group):
                re = mid[:rows, m * LANES:(m + 1) * LANES]
                im = mid[rows:, m * LANES:(m + 1) * LANES]
                blocks.append(jnp.concatenate(
                    [re * t_cos + im * t_sin, im * t_cos - re * t_sin], 1
                ).astype(BF16))
            spec = dot(jnp.concatenate(blocks, 0), g_second)
            blocks = []
            for c in range(group):
                parts = []
                for m in range(3):
                    at = (3 * c + m) * rows
                    parts.append(spec[at:at + rows, :LANES])
                    parts.append(spec[at:at + rows, LANES:])
                fr, fi, vr, vi, sr, si = parts
                blocks.append(jnp.concatenate([fr * vr - fi * vi, fr * vi + fi * vr], 1).astype(BF16))
                blocks.append(jnp.concatenate([fr * sr + fi * si, fr * si - fi * sr], 1).astype(BF16))
                blocks.append(jnp.concatenate([sr * vr + si * vi, si * vr - sr * vi], 1).astype(BF16))
            back = dot(jnp.concatenate(blocks, 0), g_third)
            flat = []
            u_cos, u_sin = t_cos * scale, t_sin * scale
            for m in range(3 * group):
                re = back[m * rows:(m + 1) * rows, :LANES]
                im = back[m * rows:(m + 1) * rows, LANES:]
                flat.append(jnp.concatenate(
                    [re * u_cos - im * u_sin, re * u_sin + im * u_cos], 0
                ).astype(BF16))
            out = dot(g_last, jnp.concatenate(flat, 1))
            for c in range(group):
                for m, ref in enumerate((conv_wide, back_wide, tapg_wide)):
                    at = (3 * c + m) * LANES
                    ref[pick(c), :] = out[:, at:at + LANES]
            return carry

        lax.fori_loop(0, part // group, some_channels, jnp.int32(0))

        biases = jnp.broadcast_to(bias[chan_lo:chan_lo + part, :], (part, LANES))
        for d in range(n_ctx):
            for j in range(tiles):
                at = (d * tiles + j) * part
                cols = slice(j * LANES, (j + 1) * LANES)
                out_send[h, d, 0, :, cols] = (
                    back_wide[at:at + part, :] + biases * sig_wide[at:at + part, :]
                ).astype(BF16)
                out_send[h, d, 1, :, cols] = (
                    conv_wide[at:at + part, :] + biases * val_wide[at:at + part, :]
                ).astype(BF16)
        for peer in ctx_peers:
            to_ctx(
                out_send.at[h, peer], out_recv.at[h, ctx],
                out_ss.at[h, peer], out_rs.at[h, ctx], peer,
            ).start()
        out_recv[h, ctx] = out_send[h, ctx]
        span = lag_tiles * part
        for e in range(n_ex):
            block = tapg_wide[e * span:(e + 1) * span, :]
            square = square + jnp.sum((block * block).reshape(span // 8, 8, LANES), 0)
            grad_send[h, e] = block.astype(BF16)
        for peer in ex_peers:
            to_ex(
                grad_send.at[h, peer], grad_recv.at[h, ex],
                grad_ss.at[h, peer], grad_rs.at[h, ex], peer,
            ).start()
        grad_recv[h, ex] = grad_send[h, ex]

    sq_send[...] = square
    for peer in ctx_peers:
        to_ctx(sq_send, sq_recv.at[ctx], sq_ss.at[peer], sq_rs.at[ctx], peer).start()
    sq_recv[ctx] = square
    for peer in ctx_peers:
        to_ctx(sq_send, sq_recv.at[peer], sq_ss.at[peer], sq_rs.at[peer], peer).wait_recv()
    total = jnp.sum(jnp.sum(sq_recv[...], 0), keepdims=True)
    rms = jnp.sqrt(total / float(rows * LANES * depth) + EPS)
    limit = bound[...].astype(F32)
    factor = jnp.broadcast_to(jnp.minimum(1.0, limit / rms), (8, LANES))
    fac_send[...] = factor
    for peer in ex_peers:
        to_ex(fac_send, fac_recv.at[ex], fac_ss.at[peer], fac_rs.at[ex], peer).start()
    fac_recv[ex] = factor
    for peer in ex_peers:
        to_ex(fac_send, fac_recv.at[peer], fac_ss.at[peer], fac_rs.at[peer], peer).wait_recv()
    for h in range(halves):
        for peer in ex_peers:
            to_ex(
                grad_send.at[h, peer], grad_recv.at[h, peer],
                grad_ss.at[h, peer], grad_rs.at[h, peer], peer,
            ).wait_recv()
        for j in range(lag_tiles):
            acc = jnp.zeros((part, LANES), F32)
            for e in range(n_ex):
                acc = acc + fac_recv[e, 0:1, :] * grad_recv[h, e, j * part:(j + 1) * part, :].astype(F32)
            filter_grad[h * part:(h + 1) * part, j * LANES:(j + 1) * LANES] = acc

    for h in range(halves):
        for peer in ctx_peers:
            to_ctx(
                out_send.at[h, peer], out_recv.at[h, peer],
                out_ss.at[h, peer], out_rs.at[h, peer], peer,
            ).wait_recv()
    turned = (((0,), (0,)), ((), ()))
    order = [(d, h) for d in range(n_ctx) for h in range(halves)]
    for lo in range(0, tokens, width):
        cols = slice(lo, lo + width)
        value_grad = stack_rows([out_recv[h, d, 0, :, cols] for d, h in order])
        state = stack_rows([out_recv[h, d, 1, :, cols] for d, h in order])
        cot = jnp.where(keep[:, cols], cotangent[0, :, cols].astype(F32), 0.0)
        gate_grad = (state.astype(F32) * cot).astype(BF16)
        result = lax.dot_general(w_value[...], value_grad, turned, preferred_element_type=F32)
        result = result + lax.dot_general(w_gate[...], gate_grad, turned, preferred_element_type=F32)
        input_grad[0, :, cols] = result.astype(BF16)

    for peer in ex_peers:
        to_ex(tap_send, tap_recv.at[ex], tap_ss.at[peer], tap_rs.at[ex], peer).wait_send()
        to_ex(fac_send, fac_recv.at[ex], fac_ss.at[peer], fac_rs.at[ex], peer).wait_send()
        for h in range(halves):
            to_ex(
                grad_send.at[h, peer], grad_recv.at[h, ex],
                grad_ss.at[h, peer], grad_rs.at[h, ex], peer,
            ).wait_send()
    for peer in ctx_peers:
        to_ctx(sq_send, sq_recv.at[ctx], sq_ss.at[peer], sq_rs.at[ctx], peer).wait_send()
        for h in range(halves):
            to_ctx(
                in_send.at[h, peer], in_recv.at[h, ctx],
                in_ss.at[h, peer], in_rs.at[h, ctx], peer,
            ).wait_send()
            to_ctx(
                out_send.at[h, peer], out_recv.at[h, ctx],
                out_ss.at[h, peer], out_rs.at[h, ctx], peer,
            ).wait_send()


def on_device(n_ctx, n_ex, stream, cotangent, ids, bound, w_value, w_gate, taps, bias):
    tokens = stream.shape[2]
    chans, lags = taps.shape
    halves = 2 if chans % 32 == 0 else 1
    part = chans // halves
    group = min(4, part)
    rows = n_ctx * tokens // LANES
    span = lags // LANES * part
    vmem = pl.BlockSpec(memory_space=pltpu.VMEM)
    dma = pltpu.SemaphoreType.DMA
    wide = pltpu.VMEM((rows * part, LANES), F32)
    across = pltpu.VMEM((halves, n_ctx, 2, part, tokens), BF16)
    return pl.pallas_call(
        functools.partial(kernel, n_ctx, n_ex, halves, group),
        out_shape=(
            jax.ShapeDtypeStruct(stream.shape, BF16),
            jax.ShapeDtypeStruct(taps.shape, F32),
        ),
        in_specs=[vmem] * 13,
        out_specs=(vmem, vmem),
        scratch_shapes=[
            across, across, across, across,
            pltpu.VMEM((chans, lags), BF16),
            pltpu.VMEM((n_ex, chans, lags), BF16),
            pltpu.VMEM((halves, n_ex, span, LANES), BF16),
            pltpu.VMEM((halves, n_ex, span, LANES), BF16),
            pltpu.VMEM((8, LANES), F32),
            pltpu.VMEM((n_ctx, 8, LANES), F32),
            pltpu.VMEM((8, LANES), F32),
            pltpu.VMEM((n_ex, 8, LANES), F32),
            wide, wide, wide, wide, wide, wide,
            dma((halves, n_ctx)), dma((halves, n_ctx)),
            dma((halves, n_ctx)), dma((halves, n_ctx)),
            dma((n_ex,)), dma((n_ex,)),
            dma((halves, n_ex)), dma((halves, n_ex)),
            dma((n_ctx,)), dma((n_ctx,)),
            dma((n_ex,)), dma((n_ex,)),
        ],
        compiler_params=pltpu.CompilerParams(collective_id=0, has_side_effects=True),
    )(
        stream, cotangent, ids, bound.reshape(1, 1), w_value, w_gate, taps, bias[:, None],
        *tables(rows),
    )


def solution(mesh):
    in_specs = (
        P("ex", None, "ctx"),
        P("ex", None, "ctx"),
        P("ex", "ctx"),
        P("ex"),
        P(),
        P(),
        P("ctx", "ex"),
        P("ctx"),
    )
    out_specs = (P("ex", None, "ctx"), P("ctx", "ex"))
    return jax.shard_map(
        functools.partial(on_device, mesh.shape["ctx"], mesh.shape["ex"]),
        mesh=mesh, in_specs=in_specs, out_specs=out_specs, check_vma=False,
    )
```

profile of v0, /device:TPU:0, one launch (start us, length us, event | category | flops | bytes accessed | tf_op | source)
XLA Modules:
  0.0 48.3 jit_solution(221957175044525347)
XLA Ops:
  1.3 0.0 copy-start.1
  1.3 0.6 %copy-done.1 = f32[32]{0:T(128)S(1)} copy-done((f32[32]{0:T(128)S(1)}, f32[32]{0:T(128)}, u32[]{:S(2)}) %copy-start.1) | copy-done | bytes 152
  1.9 0.7 %copy.15.bias = f32[32,1]{1,0:T(8,128)} copy(f32[32,1]{0,1:T(1,128)S(1)} %bitcast.3) | data formatting | bytes 256 | tf_op jit(solution)/shard_map/broadcast_in_dim | solution.py:332
  2.6 43.0 %shard_map.140 = (bf16[1,256,1024]{2,1,0:T(8,128)(2,1)}, f32[32,2048]{1,0:T(8,128)}) custom-call(bf16[1,256,1024]{2,1,0:T(8,128)(2,1)} %stream.1, bf16[1,256,1024]{2,1,0:T(8,128)(2,1)} %cotangent.1, s32[1,1024]{1,0:T(1,128)} %ids.1, s32[1,1]{1,0:T(1,128)} %bitcast.2.bound, bf16[256,256]{1,0:T(8,128)(2,1)} %w_value.1, bf16[256,256]{1,0:T(8,128)(2,1)} %w_gate.1, ...), custom_call_target="tpu_custom_call" | custom-call | tf_op jit(solution)/shard_map/pallas_call | solution.py:304
  45.7 0.0 copy-start
  45.7 1.9 %copy.19 = bf16[1,256,1024]{2,1,0:T(8,128)(2,1)} copy(bf16[1,256,1024]{2,1,0:T(8,128)(2,1)} %get-tuple-element.4) | data formatting | bytes 1048576
  47.6 0.0 copy-done
  47.6 0.7 %copy.20 = f32[32,2048]{1,0:T(8,128)} copy(f32[32,2048]{1,0:T(8,128)S(1)} %copy-done) | data formatting | bytes 524288
Async XLA Ops:
  1.3 0.7 %copy-start.1 = (f32[32]{0:T(128)S(1)}, f32[32]{0:T(128)}, u32[]{:S(2)}) copy-start(f32[32]{0:T(128)} %param.20) | copy-start | bytes 388
  45.7 1.9 %copy-start = (f32[32,2048]{1,0:T(8,128)S(1)}, f32[32,2048]{1,0:T(8,128)}, u32[]{:S(2)}) copy-start(f32[32,2048]{1,0:T(8,128)} %get-tuple-element.5) | copy-start | bytes 786436
where the time goes:
time: 48.5 us; the launch traced here: 48.3 us
  Pallas kernels  43 us (89%)
  local copies, waits for them, and re-layouts  3.96 us (8%)
  between operations  1.3 us (3%)
    pallas_call x1, Pallas kernels, on_device(): pl.pallas_call(functools.partial(kernel, n_ctx, n_ex, halves, group), out...  43 us
    unnamed x6, local copies, waits for them, and re-layouts  3.27 us

commit v1 on v0

--- a/solution.py
+++ b/solution.py
@@ -12,6 +12,7 @@
 LANES = 128
 UNKNOWN = 4
 EPS = 1e-06
+VMEM_ALL = 67043328
 F32 = jnp.float32
 BF16 = jnp.bfloat16
 MESH = pl.DeviceIdType.MESH
@@ -44,26 +45,44 @@
     return jnp.dot(x, y, preferred_element_type=F32)
 
 
-def stack_rows(blocks):
-    if blocks[0].shape[0] % 16 == 0:
-        return jnp.concatenate(blocks, 0)
-    return jnp.concatenate([b.astype(F32) for b in blocks], 0).astype(BF16)
+def partners(me, count):
+    if count & (count - 1):
+        return [lax.rem(me + i, count) for i in range(1, count)]
+    out = []
+    for i in sorted(range(1, count), key=lambda i: -bin(i >> 1).count("1")):
+        peer, bit = me, 1
+        while bit < count:
+            if i & bit:
+                peer = peer + bit - 2 * bit * lax.rem(lax.div(me, bit), 2)
+            bit *= 2
+        out.append(peer)
+    return out
 
 
 def kernel(
     n_ctx, n_ex, halves, group,
-    stream, cotangent, ids, bound, w_value, w_gate, taps, bias,
-    first, second, third, last, twist,
-    input_grad, filter_grad,
+    bound, *refs,
+):
+    sources, refs = refs[:12], refs[12:]
+    (value_grad, gate_grad, filter_sum, w_value, w_gate), refs = refs[:5], refs[5:]
+    (stream, cotangent, ids, taps, bias, first, second, third, last, twist), refs = refs[:10], refs[10:]
+    (
     in_send, in_recv, out_send, out_recv, tap_send, tap_recv, grad_send, grad_recv,
     sq_send, sq_recv, fac_send, fac_recv,
     val_wide, sig_wide, fil_wide, conv_wide, back_wide, tapg_wide,
     in_ss, in_rs, out_ss, out_rs, tap_ss, tap_rs, grad_ss, grad_rs,
-    sq_ss, sq_rs, fac_ss, fac_rs,
-):
+    sq_ss, sq_rs, fac_ss, fac_rs, load_sem,
+    ) = refs
+    held = (stream, w_value, w_gate, ids, cotangent, taps, bias, first, second, third, last, twist)
+    loads = [
+        pltpu.make_async_copy(src, dst, load_sem.at[i])
+        for i, (src, dst) in enumerate(zip(sources, held))
+    ]
+    for load in loads:
+        load.start()
     ex = lax.axis_index("ex")
     ctx = lax.axis_index("ctx")
-    ctx_peers = [lax.rem(ctx + i, n_ctx) for i in range(1, n_ctx)]
+    ctx_peers = partners(ctx, n_ctx)
     ex_peers = [lax.rem(ex + i, n_ex) for i in range(1, n_ex)]
     depth = stream.shape[1]
     tokens = stream.shape[2]
@@ -91,7 +110,10 @@
     for peer in ex_peers:
         pl.semaphore_signal(barrier, inc=1, device_id=(peer, ctx), device_id_type=MESH)
 
-    tap_send[...] = taps[...].astype(BF16)
+    for load in loads[:6]:
+        load.wait()
+    for h in range(halves):
+        tap_send[h] = taps[h * part:(h + 1) * part, :].astype(BF16)
     keep = ids[...] != UNKNOWN
 
     width = min(256, tokens)
@@ -109,19 +131,26 @@
                 in_send[h, d, 1, :, cols] = signal[at:at + part].astype(BF16)
 
     pl.semaphore_wait(barrier, n_ctx - 1 + n_ex - 1)
-    for peer in ex_peers:
-        to_ex(tap_send, tap_recv.at[ex], tap_ss.at[peer], tap_rs.at[ex], peer).start()
     for h in range(halves):
+        for peer in ex_peers:
+            to_ex(
+                tap_send.at[h], tap_recv.at[h, ex],
+                tap_ss.at[h, peer], tap_rs.at[h, ex], peer,
+            ).start()
         for peer in ctx_peers:
             to_ctx(
                 in_send.at[h, peer], in_recv.at[h, ctx],
                 in_ss.at[h, peer], in_rs.at[h, ctx], peer,
             ).start()
-    tap_recv[ex] = tap_send[...]
     for h in range(halves):
+        tap_recv[h, ex] = tap_send[h]
         in_recv[h, ctx] = in_send[h, ctx]
-    for peer in ex_peers:
-        to_ex(tap_send, tap_recv.at[peer], tap_ss.at[peer], tap_rs.at[peer], peer).wait_recv()
+    for load in loads[6:]:
+        load.wait()
+    eye = lax.broadcasted_iota(jnp.int32, (chans, chans), 0) == lax.broadcasted_iota(
+        jnp.int32, (chans, chans), 1
+    )
+    bias_col = jnp.sum(jnp.where(eye, bias[...], 0.0), 1, keepdims=True)
 
     g_first, g_second, g_third, g_last = first[...], second[...], third[...], last[...]
     scale = 1.0 / (rows * LANES)
@@ -129,17 +158,20 @@
 
     for h in range(halves):
         chan_lo = h * part
+        for peer in ctx_peers:
+            to_ctx(
+                in_send.at[h, peer], in_recv.at[h, peer],
+                in_ss.at[h, peer], in_rs.at[h, peer], peer,
+            ).wait_recv()
+        for peer in ex_peers:
+            to_ex(
+                tap_send.at[h], tap_recv.at[h, peer],
+                tap_ss.at[h, peer], tap_rs.at[h, peer], peer,
+            ).wait_recv()
         for e in range(n_ex):
             for j in range(lag_tiles):
                 at = (e * lag_tiles + j) * part
-                fil_wide[at:at + part, :] = tap_recv[
-                    e, chan_lo:chan_lo + part, j * LANES:(j + 1) * LANES
-                ].astype(F32)
-        for peer in ctx_peers:
-            to_ctx(
-                in_send.at[h, peer], in_recv.at[h, peer],
-                in_ss.at[h, peer], in_rs.at[h, peer], peer,
-            ).wait_recv()
+                fil_wide[at:at + part, :] = tap_recv[h, e, :, j * LANES:(j + 1) * LANES].astype(F32)
         for d in range(n_ctx):
             for j in range(tiles):
                 at = (d * tiles + j) * part
@@ -193,44 +225,69 @@
 
         lax.fori_loop(0, part // group, some_channels, jnp.int32(0))
 
-        biases = jnp.broadcast_to(bias[chan_lo:chan_lo + part, :], (part, LANES))
-        for d in range(n_ctx):
+        biases = jnp.broadcast_to(bias_col[chan_lo:chan_lo + part, :], (part, LANES))
+
+        def results(d):
             for j in range(tiles):
-                at = (d * tiles + j) * part
+                at = pl.ds(pl.multiple_of((d * tiles + j) * part, part), part)
                 cols = slice(j * LANES, (j + 1) * LANES)
                 out_send[h, d, 0, :, cols] = (
-                    back_wide[at:at + part, :] + biases * sig_wide[at:at + part, :]
+                    back_wide[at, :] + biases * sig_wide[at, :]
                 ).astype(BF16)
                 out_send[h, d, 1, :, cols] = (
-                    conv_wide[at:at + part, :] + biases * val_wide[at:at + part, :]
+                    conv_wide[at, :] + biases * val_wide[at, :]
                 ).astype(BF16)
+
+        def lags_out(square):
+            span = lag_tiles * part
+            for e in range(n_ex):
+                block = tapg_wide[e * span:(e + 1) * span, :]
+                square = square + jnp.sum((block * block).reshape(span // 8, 8, LANES), 0)
+                grad_send[h, e] = block.astype(BF16)
+            for peer in ex_peers:
+                to_ex(
+                    grad_send.at[h, peer], grad_recv.at[h, ex],
+                    grad_ss.at[h, peer], grad_rs.at[h, ex], peer,
+                ).start()
+            grad_recv[h, ex] = grad_send[h, ex]
+            return square
+
+        if h == halves - 1:
+            square = lags_out(square)
+            sq_send[...] = square
+            for peer in ctx_peers:
+                to_ctx(sq_send, sq_recv.at[ctx], sq_ss.at[peer], sq_rs.at[ctx], peer).start()
+            sq_recv[ctx] = square
         for peer in ctx_peers:
+            results(peer)
             to_ctx(
                 out_send.at[h, peer], out_recv.at[h, ctx],
                 out_ss.at[h, peer], out_rs.at[h, ctx], peer,
             ).start()
+        results(ctx)
         out_recv[h, ctx] = out_send[h, ctx]
-        span = lag_tiles * part
-        for e in range(n_ex):
-            block = tapg_wide[e * span:(e + 1) * span, :]
-            square = square + jnp.sum((block * block).reshape(span // 8, 8, LANES), 0)
-            grad_send[h, e] = block.astype(BF16)
-        for peer in ex_peers:
-            to_ex(
-                grad_send.at[h, peer], grad_recv.at[h, ex],
-                grad_ss.at[h, peer], grad_rs.at[h, ex], peer,
-            ).start()
-        grad_recv[h, ex] = grad_send[h, ex]
-
-    sq_send[...] = square
-    for peer in ctx_peers:
-        to_ctx(sq_send, sq_recv.at[ctx], sq_ss.at[peer], sq_rs.at[ctx], peer).start()
-    sq_recv[ctx] = square
+        if h < halves - 1:
+            square = lags_out(square)
+
+    def tokens_back(h):
+        for peer in ctx_peers:
+            to_ctx(
+                out_send.at[h, peer], out_recv.at[h, peer],
+                out_ss.at[h, peer], out_rs.at[h, peer], peer,
+            ).wait_recv()
+        for d in range(n_ctx):
+            at = d * chans + h * part
+            cot = jnp.where(keep, cotangent[0, at:at + part, :].astype(F32), 0.0)
+            value_grad[at:at + part, :] = out_recv[h, d, 0]
+            gate_grad[at:at + part, :] = (out_recv[h, d, 1].astype(F32) * cot).astype(BF16)
+
+    for h in range(halves - 1):
+        tokens_back(h)
     for peer in ctx_peers:
         to_ctx(sq_send, sq_recv.at[peer], sq_ss.at[peer], sq_rs.at[peer], peer).wait_recv()
     total = jnp.sum(jnp.sum(sq_recv[...], 0), keepdims=True)
     rms = jnp.sqrt(total / float(rows * LANES * depth) + EPS)
-    limit = bound[...].astype(F32)
+    limit = bound[0].astype(F32)
     factor = jnp.broadcast_to(jnp.minimum(1.0, limit / rms), (8, LANES))
     fac_send[...] = factor
     for peer in ex_peers:
@@ -248,30 +305,17 @@
             acc = jnp.zeros((part, LANES), F32)
             for e in range(n_ex):
                 acc = acc + fac_recv[e, 0:1, :] * grad_recv[h, e, j * part:(j + 1) * part, :].astype(F32)
-            filter_grad[h * part:(h + 1) * part, j * LANES:(j + 1) * LANES] = acc
-
-    for h in range(halves):
-        for peer in ctx_peers:
-            to_ctx(
-                out_send.at[h, peer], out_recv.at[h, peer],
-                out_ss.at[h, peer], out_rs.at[h, peer], peer,
-            ).wait_recv()
-    turned = (((0,), (0,)), ((), ()))
-    order = [(d, h) for d in range(n_ctx) for h in range(halves)]
-    for lo in range(0, tokens, width):
-        cols = slice(lo, lo + width)
-        value_grad = stack_rows([out_recv[h, d, 0, :, cols] for d, h in order])
-        state = stack_rows([out_recv[h, d, 1, :, cols] for d, h in order])
-        cot = jnp.where(keep[:, cols], cotangent[0, :, cols].astype(F32), 0.0)
-        gate_grad = (state.astype(F32) * cot).astype(BF16)
-        result = lax.dot_general(w_value[...], value_grad, turned, preferred_element_type=F32)
-        result = result + lax.dot_general(w_gate[...], gate_grad, turned, preferred_element_type=F32)
-        input_grad[0, :, cols] = result.astype(BF16)
+            filter_sum[h * part:(h + 1) * part, j * LANES:(j + 1) * LANES] = acc
+
+    tokens_back(halves - 1)
 
     for peer in ex_peers:
-        to_ex(tap_send, tap_recv.at[ex], tap_ss.at[peer], tap_rs.at[ex], peer).wait_send()
         to_ex(fac_send, fac_recv.at[ex], fac_ss.at[peer], fac_rs.at[ex], peer).wait_send()
         for h in range(halves):
+            to_ex(
+                tap_send.at[h], tap_recv.at[h, ex],
+                tap_ss.at[h, peer], tap_rs.at[h, ex], peer,
+            ).wait_send()
             to_ex(
                 grad_send.at[h, peer], grad_recv.at[h, ex],
                 grad_ss.at[h, peer], grad_rs.at[h, ex], peer,
@@ -287,6 +331,18 @@
                 out_send.at[h, peer], out_recv.at[h, ctx],
                 out_ss.at[h, peer], out_rs.at[h, ctx], peer,
             ).wait_send()
+
+
+def finish(value_grad, gate_grad, w_value, w_gate, filter_sum, input_grad, filter_grad):
+    turned = (((0,), (0,)), ((), ()))
+    filter_grad[...] = filter_sum[...]
+    tokens = value_grad.shape[1]
+    width = min(256, tokens)
+    for lo in range(0, tokens, width):
+        cols = slice(lo, lo + width)
+        result = lax.dot_general(w_value[...], value_grad[:, cols], turned, preferred_element_type=F32)
+        result = result + lax.dot_general(w_gate[...], gate_grad[:, cols], turned, preferred_element_type=F32)
+        input_grad[0, :, cols] = result.astype(BF16)
 
 
 def on_device(n_ctx, n_ex, stream, cotangent, ids, bound, w_value, w_gate, taps, bias):
@@ -301,18 +357,26 @@
     dma = pltpu.SemaphoreType.DMA
     wide = pltpu.VMEM((rows * part, LANES), F32)
     across = pltpu.VMEM((halves, n_ctx, 2, part, tokens), BF16)
-    return pl.pallas_call(
+    depth = stream.shape[1]
+    operands = (
+        stream, w_value, w_gate, ids, cotangent, taps, bias.reshape(1, -1), *tables(rows),
+    )
+    loaded = [pltpu.VMEM(operands[i].shape, operands[i].dtype) for i in (0, 4, 3, 5, 6, 7, 8, 9, 10, 11)]
+    value_grad, gate_grad, filter_sum, w_value, w_gate = pl.pallas_call(
         functools.partial(kernel, n_ctx, n_ex, halves, group),
         out_shape=(
-            jax.ShapeDtypeStruct(stream.shape, BF16),
+            jax.ShapeDtypeStruct((depth, tokens), BF16),
+            jax.ShapeDtypeStruct((depth, tokens), BF16),
             jax.ShapeDtypeStruct(taps.shape, F32),
+            jax.ShapeDtypeStruct(w_value.shape, w_value.dtype),
+            jax.ShapeDtypeStruct(w_gate.shape, w_gate.dtype),
         ),
-        in_specs=[vmem] * 13,
-        out_specs=(vmem, vmem),
-        scratch_shapes=[
+        in_specs=[pl.BlockSpec(memory_space=pltpu.SMEM)] + [pl.BlockSpec(memory_space=pltpu.HBM)] * 12,
+        out_specs=(vmem,) * 5,
+        scratch_shapes=loaded + [
             across, across, across, across,
-            pltpu.VMEM((chans, lags), BF16),
-            pltpu.VMEM((n_ex, chans, lags), BF16),
+            pltpu.VMEM((halves, part, lags), BF16),
+            pltpu.VMEM((halves, n_ex, part, lags), BF16),
             pltpu.VMEM((halves, n_ex, span, LANES), BF16),
             pltpu.VMEM((halves, n_ex, span, LANES), BF16),
             pltpu.VMEM((8, LANES), F32),
@@ -322,16 +386,24 @@
             wide, wide, wide, wide, wide, wide,
             dma((halves, n_ctx)), dma((halves, n_ctx)),
             dma((halves, n_ctx)), dma((halves, n_ctx)),
-            dma((n_ex,)), dma((n_ex,)),
+            dma((halves, n_ex)), dma((halves, n_ex)),
             dma((halves, n_ex)), dma((halves, n_ex)),
             dma((n_ctx,)), dma((n_ctx,)),
             dma((n_ex,)), dma((n_ex,)),
+            dma((12,)),
         ],
-        compiler_params=pltpu.CompilerParams(collective_id=0, has_side_effects=True),
-    )(
-        stream, cotangent, ids, bound.reshape(1, 1), w_value, w_gate, taps, bias[:, None],
-        *tables(rows),
-    )
+        compiler_params=pltpu.CompilerParams(collective_id=0, has_side_effects=True, vmem_limit_bytes=VMEM_ALL),
+    )(bound, *operands)
+    return pl.pallas_call(
+        finish,
+        out_shape=(
+            jax.ShapeDtypeStruct(stream.shape, BF16),
+            jax.ShapeDtypeStruct(taps.shape, F32),
+        ),
+        in_specs=[vmem] * 5,
+        out_specs=(vmem, vmem),
+        compiler_params=pltpu.CompilerParams(vmem_limit_bytes=VMEM_ALL),
+    )(value_grad, gate_grad, w_value, w_gate, filter_sum)
 
 
 def solution(mesh):

time: 48.5 us -> 38.9 us (0.80)
  Pallas kernels: 43 us -> 37.5 us
  local copies, waits for them, and re-layouts: 3.96 us -> 0 us
    pallas_call x1, Pallas kernels: 43 us -> 34.8 us  [on_device(): pl.pallas_call(functools.partial(kernel, n_ctx, n_ex, halves, group), out...]
    unnamed x6 -> x0, local copies, waits for them, and re-layouts: 3.27 us -> none
    pallas_call x0 -> x1, Pallas kernels: none -> 2.65 us  [on_device(): pl.pallas_call(finish, out_shape=(jax.ShapeDtypeStruct(stream.shape, BF16...]
    broadcast_in_dim x1 -> x0, local copies, waits for them, and re-layouts: 0.69 us -> none  [on_device(): bias[:, None]]
where the time goes in v1:
time: 38.9 us; the launch traced here: 38.7 us
  Pallas kernels  37.5 us (96%)
  between operations  1.29 us (3%)
    pallas_call x1, Pallas kernels, on_device(): pl.pallas_call(functools.partial(kernel, n_ctx, n_ex, halves, group), out...  34.8 us
    pallas_call x1, Pallas kernels, on_device(): pl.pallas_call(finish, out_shape=(jax.ShapeDtypeStruct(stream.shape, BF16...  2.65 us

profile of v1, /device:TPU:0, one launch (start us, length us, event | category | flops | bytes accessed | tf_op | source)
XLA Modules:
  0.0 38.7 jit_solution(8041840882716481939)
XLA Ops:
  1.3 34.8 %shard_map.140 = (bf16[256,1024]{1,0:T(8,128)(2,1)}, bf16[256,1024]{1,0:T(8,128)(2,1)}, f32[32,2048]{1,0:T(8,128)}, bf16[256,256]{1,0:T(8,128)(2,1)}, bf16[256,256]{1,0:T(8,128)(2,1)}) custom-call(s32[1]{0:T(128)S(6)} %copy.15.bound, bf16[1,256,1024]{2,1,0:T(8,128)(2,1)} %refs_0_.1, bf16[256,256]{1,0:T(8,128)(2,1)} %refs_1_.1, bf16[256,256]{1,0:T(8,128)(2,1)} %refs_2_.1, ...), custom_call_target="tpu_custom_call" | custom-call | tf_op jit(solution)/shard_map/pallas_call | solution.py:365
  36.1 2.7 %shard_map.141 = (bf16[1,256,1024]{2,1,0:T(8,128)(2,1)}, f32[32,2048]{1,0:T(8,128)}) custom-call(bf16[256,1024]{1,0:T(8,128)(2,1)} %get-tuple-element.7.value_grad, bf16[256,1024]{1,0:T(8,128)(2,1)} %get-tuple-element.8.gate_grad, bf16[256,256]{1,0:T(8,128)(2,1)} %get-tuple-element.9.w_value, bf16[256,256]{1,0:T(8,128)(2,1)} %get-tuple-element.10.w_gate, ...), custom_call_target="tpu_custom_call" | custom-call | tf_op jit(solution)/shard_map/pallas_call | solution.py:397

commit v2 on v1

--- a/solution.py
+++ b/solution.py
@@ -350,7 +350,7 @@
     chans, lags = taps.shape
     halves = 2 if chans % 32 == 0 else 1
     part = chans // halves
-    group = min(4, part)
+    group = min(8, part)
     rows = n_ctx * tokens // LANES
     span = lags // LANES * part
     vmem = pl.BlockSpec(memory_space=pltpu.VMEM)

time: 38.9 us -> 38.2 us (0.982)
  Pallas kernels: 37.5 us -> 36.8 us
    pallas_call x1, Pallas kernels: 34.8 us -> 34.1 us  [on_device(): pl.pallas_call(functools.partial(kernel, n_ctx, n_ex, halves, group), out...]
where the time goes in v2:
time: 38.2 us; the launch traced here: 38 us
  Pallas kernels  36.8 us (96%)
  between operations  1.29 us (3%)
    pallas_call x1, Pallas kernels, on_device(): pl.pallas_call(functools.partial(kernel, n_ctx, n_ex, halves, group), out...  34.1 us
    pallas_call x1, Pallas kernels, on_device(): pl.pallas_call(finish, out_shape=(jax.ShapeDtypeStruct(stream.shape, BF16...  2.65 us

profile of v2, /device:TPU:0, one launch (start us, length us, event | category | flops | bytes accessed | tf_op | source)
XLA Modules:
  0.0 38.0 jit_solution(2708311808134600881)
XLA Ops:
  1.3 34.1 %shard_map.140 = (bf16[256,1024]{1,0:T(8,128)(2,1)}, bf16[256,1024]{1,0:T(8,128)(2,1)}, f32[32,2048]{1,0:T(8,128)}, bf16[256,256]{1,0:T(8,128)(2,1)}, bf16[256,256]{1,0:T(8,128)(2,1)}) custom-call(s32[1]{0:T(128)S(6)} %copy.15.bound, bf16[1,256,1024]{2,1,0:T(8,128)(2,1)} %refs_0_.1, bf16[256,256]{1,0:T(8,128)(2,1)} %refs_1_.1, bf16[256,256]{1,0:T(8,128)(2,1)} %refs_2_.1, ...), custom_call_target="tpu_custom_call" | custom-call | tf_op jit(solution)/shard_map/pallas_call | solution.py:365
  35.4 2.7 %shard_map.141 = (bf16[1,256,1024]{2,1,0:T(8,128)(2,1)}, f32[32,2048]{1,0:T(8,128)}) custom-call(bf16[256,1024]{1,0:T(8,128)(2,1)} %get-tuple-element.7.value_grad, bf16[256,1024]{1,0:T(8,128)(2,1)} %get-tuple-element.8.gate_grad, bf16[256,256]{1,0:T(8,128)(2,1)} %get-tuple-element.9.w_value, bf16[256,256]{1,0:T(8,128)(2,1)} %get-tuple-element.10.w_gate, ...), custom_call_target="tpu_custom_call" | custom-call | tf_op jit(solution)/shard_map/pallas_call | solution.py:397
